TPU v7x, 256 devices: a whole 4x4x8 slice. The times are simulated.
256 devices in a mesh: seq: 16 (over x_hi, y, core), heads: 16 (over z, x_lo).
Axes of the slice: x: 4 (x_hi: 2, x_lo: 2; x = x_hi * 2 + x_lo), y: 4, z: 8, core: 2. Of those that a mesh axis runs over, the one named last changes fastest.
Arguments:
- activations: bfloat16 [12288, 4096], P('seq', 'heads'), may hold values from -24 to 24
- w_query: bfloat16 [4096, 4096], P(None, 'heads'), may hold values from -0.1875 to 0.1875
- w_key: bfloat16 [4096, 4096], P(None, 'heads'), may hold values from -0.09375 to 0.09375
- w_value: bfloat16 [4096, 4096], P(None, 'heads'), may hold values from -0.09375 to 0.09375
- w_out: bfloat16 [4096, 4096], P('heads'), may hold values from -0.1875 to 0.1875
- windows: int32 [32], P('heads'), may hold values from 1 to 2, as said below
- rand_blocks: int32 [96, 3], P('seq'), may hold values from 0 to 95, as said below
- global_pos: int32 [128], replicated, may hold values from 0 to 12287, as said below
Outputs:
- attended: bfloat16 [12288, 4096], P('seq', 'heads')
Inputs may be any that keep to these rules, and one draw needn't show every extreme that they name: `windows`: some head has reach 2. `rand_blocks`: the 3 entries of a row are distinct. Of the 18 entries in the rows of one index of seq, at most 2 fall into the 6 blocks of any one index, and exactly 2 into those of some index. `global_pos`: Distinct. At most 32 fall into the 768 positions of one index of seq, and exactly 32 into those of some index.
All inputs are finite; a program needn't handle non-finite values.
Results may differ from a plain program's by a relative error of at most 0.024.
The roundings to bfloat16 on the way count: a program that leaves them out, or rounds other values in their place, can miss the bound.
Values may be sent and summed in bfloat16 or wider, within the bound.
No kernel may reach another device: no remote copies, remote signals or barrier semaphores. Data moves between devices by JAX's collectives and lax.ppermute only.
A program may use at most 128 MiB of HBM per device.

v0:
```python
import math
import jax
import jax.numpy as jnp
from jax import lax
from jax.sharding import PartitionSpec as P

WMAX = 2
NEGATIVE = -1e30


def extended(block, sides, width):
    for axis, dim in sides:
        count = lax.axis_size(axis)
        forward = [(i, i + 1) for i in range(count - 1)]
        forward.append((count - 1, 0))
        backward = [(target, source) for source, target in forward]
        low = lax.ppermute(
            lax.slice_in_dim(block, block.shape[dim] - width, None, axis=dim), axis, forward
        )
        high = lax.ppermute(lax.slice_in_dim(block, 0, width, axis=dim), axis, backward)
        block = jnp.concatenate([low, block, high], axis=dim)
    return block


def combined_all(value, axis, join):
    pieces = jax.tree.map(lambda part: lax.all_gather(part, axis), value)
    head = jax.tree.map(lambda part: part[0], pieces)
    tail = jax.tree.map(lambda part: part[1:], pieces)
    running, _ = lax.scan(lambda running, slab: (join(running, slab), None), head, tail)
    return running


def fold_scores(state, scores, valid):
    top_old, sum_old, acc_old = state
    masked = jnp.where(valid, scores, NEGATIVE)
    top_new = jnp.maximum(top_old, jnp.max(masked, axis=-1))
    probs = jnp.where(valid, jnp.exp(masked - top_new[..., None]), 0.0)
    keep = jnp.exp(top_old - top_new)
    return (
        top_new,
        keep * sum_old + jnp.sum(probs, axis=-1),
        keep[..., None] * acc_old,
        probs.astype(jnp.bfloat16),
    )


def join_states(first, second):
    top_first, sum_first, acc_first = first
    top_second, sum_second, acc_second = second
    top_both = jnp.maximum(top_first, top_second)
    keep_first = jnp.exp(top_first - top_both)
    keep_second = jnp.exp(top_second - top_both)
    return (
        top_both,
        keep_first * sum_first + keep_second * sum_second,
        keep_first[..., None] * acc_first + keep_second[..., None] * acc_second,
    )


def on_device(activations, w_query, w_key, w_value, w_out, windows, rand_blocks, global_pos):
    rows_here = activations.shape[0]
    group_width = w_query.shape[1]
    heads_here = windows.shape[0]
    head_size = group_width // heads_here
    blocks_here = rand_blocks.shape[0]
    block_rows = rows_here // blocks_here
    picks_per_block = rand_blocks.shape[1]
    seq_count = lax.axis_size("seq")
    position = lax.axis_index("seq")
    score_scale = 1.0 / math.sqrt(head_size)
    piece = lax.all_gather(activations, "heads", axis=1, tiled=True)
    sums_query = jnp.dot(piece, w_query, preferred_element_type=jnp.float32)
    sums_key = jnp.dot(piece, w_key, preferred_element_type=jnp.float32)
    sums_value = jnp.dot(piece, w_value, preferred_element_type=jnp.float32)
    query = sums_query.astype(jnp.bfloat16)
    keys = sums_key.astype(jnp.bfloat16)
    values = sums_value.astype(jnp.bfloat16)
    query_blocks = query.reshape(blocks_here, block_rows, heads_here, head_size)
    stacked = jnp.stack([keys, values], 0)
    padded = extended(stacked, (("seq", 1),), WMAX * block_rows)
    span = 2 * WMAX + 1
    padded_blocks = padded.reshape(2, blocks_here + 2 * WMAX, block_rows, heads_here, head_size)
    window_kv = jnp.concatenate(
        [padded_blocks[:, offset : offset + blocks_here, None] for offset in range(span)], axis=2
    )
    window_kv = window_kv.reshape(2, blocks_here, span * block_rows, heads_here, head_size)
    distance = jnp.abs(jnp.arange(span, dtype=jnp.int32) - WMAX)
    window_valid = jnp.repeat(distance[None, :] <= windows[:, None], block_rows, axis=1)[
        None, :, None, :
    ]
    scores = (
        jnp.einsum(
            "bqhd,bkhd->bhqk", query_blocks, window_kv[0], preferred_element_type=jnp.float32
        )
        * score_scale
    )
    start_state = (
        jnp.full((blocks_here, heads_here, block_rows), NEGATIVE, jnp.float32),
        jnp.zeros((blocks_here, heads_here, block_rows), jnp.float32),
        jnp.zeros((blocks_here, heads_here, block_rows, head_size), jnp.float32),
    )
    top, total, accum, attention_weights = fold_scores(start_state, scores, window_valid)
    accum = jnp.einsum(
        "bhqk,bkhd->bhqd", attention_weights, window_kv[1], preferred_element_type=jnp.float32
    )
    state = (top, total, accum)
    all_valid = jnp.ones((1, 1, 1, 1), dtype=bool)
    targets = rand_blocks.reshape(-1)
    request_count = targets.shape[0]
    sources = targets // blocks_here
    order = jnp.arange(request_count, dtype=jnp.int32)
    earlier = (sources[:, None] == sources[None, :]) & (order[None, :] < order[:, None])
    ranks = jnp.sum(earlier.astype(jnp.int32), axis=1)
    slot_count = (request_count + seq_count - 1) // seq_count
    hits = (sources[:, None, None] == jnp.arange(seq_count, dtype=jnp.int32)[None, :, None]) & (
        ranks[:, None, None] == jnp.arange(slot_count, dtype=jnp.int32)[None, None, :]
    )
    slot_request = jnp.sum(jnp.where(hits, order[:, None, None], 0), axis=0)
    slot_live = jnp.any(hits, axis=0)
    row_steps = jnp.arange(block_rows, dtype=jnp.int32)
    owner_ids = jnp.arange(blocks_here, dtype=jnp.int32)
    piece = lax.all_gather(stacked, "seq", axis=1, tiled=True)
    count = piece.shape[1]
    picked = slot_request.reshape(-1)
    alive = slot_live.reshape(-1)
    slot_total = picked.shape[0]
    offset_rows = targets[picked][:, None] * block_rows + row_steps[None, :]
    chosen = piece[:, jnp.clip(offset_rows, 0, count - 1).reshape(-1)]
    chosen = chosen.reshape(2, slot_total * block_rows, heads_here, head_size)
    part_scores = (
        jnp.einsum("bqhd,khd->bhqk", query_blocks, chosen[0], preferred_element_type=jnp.float32)
        * score_scale
    )
    belongs = alive[None, :] & ((picked // picks_per_block)[None, :] == owner_ids[:, None])
    valid = jnp.repeat(belongs, block_rows, axis=1)[:, None, None, :]
    top_new, total_new, accum_new, part_weights = fold_scores(state, part_scores, valid)
    state = (
        top_new,
        total_new,
        accum_new
        + jnp.einsum("bhqk,khd->bhqd", part_weights, chosen[1], preferred_element_type=jnp.float32),
    )
    global_count = global_pos.shape[0]
    local_pos = global_pos - position * rows_here
    owned = (local_pos >= 0) & (local_pos < rows_here)
    row_ids = jnp.arange(rows_here, dtype=jnp.int32)
    selector = owned[:, None] & (local_pos[:, None] == row_ids[None, :])
    projected = jnp.concatenate([query, keys, values], axis=1)
    chosen_rows = jnp.dot(
        selector.astype(jnp.bfloat16), projected, preferred_element_type=jnp.float32
    )
    shared = lax.psum(chosen_rows.astype(jnp.bfloat16), "seq")
    g_query = shared[:, :group_width].reshape(global_count, heads_here, head_size)
    g_key = shared[:, group_width : 2 * group_width].reshape(global_count, heads_here, head_size)
    g_value = shared[:, 2 * group_width :].reshape(global_count, heads_here, head_size)
    global_score_rows = (
        jnp.einsum("bqhd,ghd->bhqg", query_blocks, g_key, preferred_element_type=jnp.float32)
        * score_scale
    )
    top, total, accum, attention_weights = fold_scores(state, global_score_rows, all_valid)
    accum = accum + jnp.einsum(
        "bhqg,ghd->bhqd", attention_weights, g_value, preferred_element_type=jnp.float32
    )
    sparse = (accum / total[..., None]).transpose(0, 2, 1, 3).reshape(rows_here, group_width)
    key_heads = keys.reshape(rows_here, heads_here, head_size)
    value_heads = values.reshape(rows_here, heads_here, head_size)
    g_scores = (
        jnp.einsum("ghd,thd->hgt", g_query, key_heads, preferred_element_type=jnp.float32)
        * score_scale
    )
    g_top = jnp.max(g_scores, axis=-1)
    g_probs = jnp.exp(g_scores - g_top[..., None])
    g_total = jnp.sum(g_probs, axis=-1)
    g_accum = jnp.einsum(
        "hgt,thd->hgd",
        g_probs.astype(jnp.bfloat16),
        value_heads,
        preferred_element_type=jnp.float32,
    )
    merged_top, merged_total, merged_accum = combined_all(
        (g_top, g_total, g_accum), "seq", join_states
    )
    finished = merged_accum / merged_total[..., None]
    placing = selector.astype(jnp.float32).T
    placed = jnp.einsum("tg,hgd->thd", placing, finished, precision=lax.Precision.HIGHEST)
    is_global = jnp.sum(placing, axis=1) > 0.5
    context = jnp.where(is_global[:, None], placed.reshape(rows_here, group_width), sparse).astype(
        jnp.bfloat16
    )
    term = jnp.dot(context, w_out, preferred_element_type=jnp.float32)
    return lax.psum_scatter(term.astype(jnp.bfloat16), "heads", scatter_dimension=1, tiled=True)


def solution(mesh):
    in_specs = (
        P("seq", "heads"),
        P(None, "heads"),
        P(None, "heads"),
        P(None, "heads"),
        P("heads", None),
        P("heads"),
        P("seq", None),
        P(),
    )
    out_specs = P("seq", "heads")
    return jax.shard_map(
        on_device, mesh=mesh, in_specs=in_specs, out_specs=out_specs, check_vma=False
    )
```

profile of v0, /device:TPU:1, one launch (start us, length us, event | category | flops | bytes accessed | tf_op | source)
XLA Modules:
  0.0 761.6 jit_solution(3525437572789591166)
XLA Ops:
  6.5 0.7 all-gather.9.cloned.1.call-update
  7.3 0.7 compare_and_fusion.1
  8.0 157.4 %all-gather.9.cloned.1.call-done = bf16[768,4096]{1,0:T(8,128)(2,1)} async-done(((bf16[768,256]{1,0:T(8,128)(2,1)}), bf16[768,4096]{1,0:T(8,128)(2,1)}) %all-gather.9.cloned.1.call-update) | async-done | bytes 6291472 | tf_op jit(solution)/shard_map/all_gather | solution.py:71
  165.4 5.4 convolution_convert_fusion.1
  171.2 2.0 convolution_convert_fusion.2
  173.2 2.0 convolution_convert_fusion.3
  175.2 1.2 fusion.43
  176.5 143.8 %all-reduce.2.cloned.1.call-done = bf16[128,768]{1,0:T(8,128)(2,1)} async-done(((bf16[128,768]{1,0:T(8,128)(2,1)}), bf16[128,768]{1,0:T(8,128)(2,1)}) %all-reduce.2.cloned.1.call-update) | async-done | bytes 196624 | tf_op jit(solution)/shard_map/psum | solution.py:152
  320.3 1.6 fusion.95
  321.9 1.3 fusion.96
  323.2 1.0 fusion.55
  324.3 2.0 pad_maximum_fusion.1
  328.4 0.7 gather_fusion
  329.4 0.6 copy.235
  331.4 1.9 copy.142
  333.4 1.8 reshape.309
  335.2 1.8 fusion.67
  337.5 2.0 collective-permute-start.1
  339.5 26.6 %all-gather.3 = f32[16,2,128]{2,1,0:T(2,128)S(1)} all-gather(f32[1,2,128]{2,1,0:T(2,128)S(1)} %bitcast.208), channel_id=2, replica_groups=mesh['seq'=16,'heads'=16] {'seq'}, dimensions={0}, use_global_device_ids=true | all-gather | bytes 17408 | tf_op jit(solution)/shard_map/all_gather | solution.py:26
  366.4 19.3 %all-gather.4 = f32[16,2,128]{2,1,0:T(2,128)S(1)} all-gather(f32[1,2,128]{2,1,0:T(2,128)S(1)} %bitcast.209), channel_id=3, replica_groups=mesh['seq'=16,'heads'=16] {'seq'}, dimensions={0}, use_global_device_ids=true | all-gather | bytes 17408 | tf_op jit(solution)/shard_map/all_gather | solution.py:26
  386.2 1.6 copy.187
  387.8 0.9 reshape.313
  388.6 2.2 fusion.97
  390.8 2.3 pad_maximum_fusion
  393.1 2.5 copy.143
  395.6 3.0 reshape.310
  398.6 0.7 fusion.50
  399.2 0.7 fusion.49
  400.0 0.7 fusion.48
  400.7 0.7 fusion.47
  401.4 0.7 fusion.46
  402.2 4.7 fusion.94
  406.9 1.8 copy.159
  409.2 2.7 fusion.8
  411.9 3.0 slice.104
  415.0 16.8 %while.14 = (s32[]{:T(128)}, f32[2,128]{1,0:T(2,128)S(1)}, f32[2,128]{1,0:T(2,128)S(1)}, f32[2,128,128]{2,1,0:T(8,128)S(1)}, f32[15,2,128]{2,1,0:T(2,128)S(1)}, ...) while((s32[]{:T(128)}, f32[2,128]{1,0:T(2,128)S(1)}, f32[2,128]{1,0:T(2,128)S(1)}, ...), condition=%wide.region_5.6_spmd, body=%wide.region_4.5_spmd.sunk | while | flops 99842 | bytes 403557 | solution.py:29
  415.0 1.1 fusion.117
  416.1 1.1 fusion.117
  417.2 1.1 fusion.117
  418.4 1.1 fusion.117
  419.5 1.1 fusion.117
  420.6 1.1 fusion.117
  421.7 1.1 fusion.117
  422.8 1.1 fusion.117
  423.9 1.1 fusion.117
  425.0 1.1 fusion.117
  426.2 1.1 fusion.117
  427.4 1.1 fusion.117
  428.5 1.1 fusion.117
  429.6 1.1 fusion.117
  430.7 1.1 fusion.117
  432.0 45.2 %all-gather.11.cloned.1.call-done = bf16[2,12288,256]{1,2,0:T(8,128)(2,1)} async-done(((bf16[2,768,256]{1,2,0:T(8,128)(2,1)}), bf16[2,12288,256]{1,2,0:T(8,128)(2,1)}) %all-gather.11.cloned.1.call-update) | async-done | bytes 12582928 | tf_op jit(solution)/shard_map/all_gather | solution.py:122
  477.2 30.9 %copy.151 = bf16[2,12288,256]{2,0,1:T(2,128)(2,1)} copy(bf16[2,12288,256]{1,2,0:T(8,128)(2,1)} %all-gather.11.cloned.1.call-done) | data formatting | bytes 25165824 | tf_op jit(solution)/shard_map/all_gather | solution.py:122
  508.2 37.2 %gather_fusion.1 = bf16[4096,2,256]{2,1,0:T(2,128)(2,1)} fusion(bf16[2,12288,256]{2,0,1:T(2,128)(2,1)} %copy.151, s32[4096]{0:T(1024)S(1)} %copy-done.8), kind=kCustom, calls=%fused_computation.1 | custom fusion | bytes 8404992 | tf_op jit(solution)/shard_map/gather | solution.py:128
  545.3 9.9 %fusion.93 = (bf16[1,4096,256]{2,0,1:T(2,128)(2,1)}, bf16[1,4096,256]{2,0,1:T(2,128)(2,1)}) fusion(bf16[2,4096,256]{2,0,1:T(2,128)(2,1)} %bitcast.183), kind=kLoop, calls=%fused_computation.149 | loop fusion | bytes 8388608 | tf_op jit(solution)/shard_map/slice | solution.py:131
  555.2 9.8 %copy.152 = bf16[1,4096,256]{1,2,0:T(8,128)(2,1)} copy(bf16[1,4096,256]{2,0,1:T(2,128)(2,1)} %get-tuple-element.72) | data formatting | bytes 4194304 | tf_op jit(solution)/shard_map/slice | solution.py:131
  565.0 9.8 %copy.160 = bf16[1,4096,256]{1,2,0:T(8,128)(2,1)} copy(bf16[1,4096,256]{2,0,1:T(2,128)(2,1)} %get-tuple-element.73) | data formatting | bytes 4194304 | tf_op jit(solution)/shard_map/slice | solution.py:141
  574.8 7.7 %fusion.3 = (f32[6,2,128]{2,0,1:T(8,128)S(1)}, f32[2,4096,6,128]{3,1,2,0:T(8,128)S(1)}) fusion(pred[6,4096]{1,0:T(8,128)(4,1)S(1)} %bitcast.199, bf16[4096,2,128,1]{0,2,3,1:T(8,128)(2,1)} %bitcast.195, bf16[6,128,2,128]{3,2,1,0:T(2,128)(2,1)S(1)} %copy-done.3), kind=kOutput, calls=%fused_computation.13 | convolution fusion | flops 1629485568 | bytes 27686912 | tf_op jit(solution)/shard_map/bqhd,khd->bhqk/dot_general | solution.py:131
  582.7 1.2 fusion.9
  583.9 13.8 %fusion.4 = (f32[6,2,128]{2,0,1:T(8,128)S(1)}, bf16[6,2,128,4096]{2,3,0,1:T(8,128)(2,1)}) fusion(f32[2,4096,6,128]{3,1,2,0:T(8,128)S(1)} %get-tuple-element.89, f32[6,2,128]{2,0,1:T(8,128)S(1)} %copy.162, pred[6,4096]{1,0:T(8,128)(4,1)S(1)} %bitcast.200), kind=kLoop, calls=%fused_computation.14 | loop fusion | flops 37747200 | bytes 37785600 | tf_op jit(solution)/shard_map/reduce_sum | solution.py:41
  597.7 10.6 %fusion.18 = f32[6,128,2,128]{3,1,2,0:T(8,128)} fusion(bf16[4096,2,128,1]{0,2,1,3:T(8,128)(2,1)S(1)} %bitcast.194, bf16[6,2,128,4096]{2,3,0,1:T(8,128)(2,1)} %get-tuple-element.71), kind=kOutput, calls=%fused_computation.31 | convolution fusion | flops 1610612736 | bytes 15466496 | tf_op jit(solution)/shard_map/bhqk,khd->bhqd/dot_general | solution.py:141
  608.3 3.2 fusion.33
  613.0 4.5 convolution_convert_fusion
  617.5 137.5 %reduce-scatter.2.cloned.1.call-done = bf16[768,256]{1,0:T(8,128)(2,1)} async-done(((bf16[768,4096]{1,0:T(8,128)(2,1)}), bf16[768,256]{1,0:T(8,128)(2,1)}) %reduce-scatter.2.cloned.1.call-update) | async-done | bytes 393232 | tf_op jit(solution)/shard_map/reduce_scatter | solution.py:191
  (129 shorter events, 8.4 us)
Async XLA Ops:
  6.5 606.5 %copy-start = (bf16[256,4096]{1,0:T(8,128)(2,1)S(1)}, bf16[256,4096]{1,0:T(8,128)(2,1)}, u32[]{:S(2)}) copy-start(bf16[256,4096]{1,0:T(8,128)(2,1)} %param.14) | copy-start | bytes 6291460
  6.5 158.8 %all-gather.9.cloned.1.call-start = ((), (), s32[]{:S(2)}) async-start(), calls=%async_computation.1 | async-start | bytes 6684672 | tf_op jit(solution)/shard_map/all_gather | solution.py:71
  7.3 313.1 %all-reduce.2.cloned.1.call-start = ((), (), s32[]{:S(2)}) async-start(), calls=%async_computation.2 | async-start | bytes 393216 | tf_op jit(solution)/shard_map/psum | solution.py:152
  8.0 322.1 %copy-start.15 = (pred[128]{0:T(512)(128)(4,1)}, pred[128]{0:T(512)(128)(4,1)S(1)}, u32[]{:S(2)}) copy-start(pred[128]{0:T(512)(128)(4,1)S(1)} %get-tuple-element.68) | copy-start | bytes 388
  8.0 322.1 %copy-start.17 = (s32[128]{0:T(128)}, s32[128]{0:T(128)S(1)}, u32[]{:S(2)}) copy-start(s32[128]{0:T(128)S(1)} %get-tuple-element.69) | copy-start | bytes 1540
  165.4 5.4 copy-start.20
  165.4 5.8 copy-start.21
  171.2 2.0 copy-start.22
  173.2 2.0 copy-start.2
  175.2 146.7 %copy-start.6 = (bf16[768,256]{0,1:T(8,128)(2,1)}, bf16[768,256]{0,1:T(8,128)(2,1)S(1)}, u32[]{:S(2)}) copy-start(bf16[768,256]{0,1:T(8,128)(2,1)S(1)} %convolution_convert_fusion.3) | copy-start | bytes 1179652
  175.2 151.2 %copy-start.23 = (s32[2]{0:T(128)S(1)}, s32[2]{0:T(128)}, u32[]{:S(2)}) copy-start(s32[2]{0:T(128)} %param.15) | copy-start | bytes 28
  175.2 151.9 %copy-start.14 = (s32[6,3]{0,1:T(4,128)S(1)}, s32[6,3]{0,1:T(4,128)}, u32[]{:S(2)}) copy-start(s32[6,3]{0,1:T(4,128)} %param.16) | copy-start | bytes 220
  176.5 235.4 %all-gather.13.cloned.1.call-start = ((), (), s32[]{:S(2)}) async-start(), calls=%async_computation.5 | async-start | bytes 2228224 | tf_op jit(solution)/shard_map/all_gather | solution.py:26
  324.3 152.9 %all-gather.11.cloned.1.call-start = ((), (), s32[]{:S(2)}) async-start(), calls=%async_computation.3 | async-start | bytes 13369344 | tf_op jit(solution)/shard_map/all_gather | solution.py:122
  326.3 428.7 %reduce-scatter.2.cloned.1.call-start = ((), (), s32[]{:S(2)}) async-start(), calls=%async_computation.4 | async-start | bytes 6684672 | tf_op jit(solution)/shard_map/reduce_scatter | solution.py:191
  337.0 53.8 %collective-permute-start = (bf16[2,256,256]{1,2,0:T(8,128)(2,1)}, bf16[2,256,256]{1,2,0:T(8,128)(2,1)S(1)}, u32[]{:S(2)}, u32[]{:S(2)}) collective-permute-start(bf16[2,256,256]{1,2,0:T(8,128)(2,1)} %get-tuple-element.78), channel_id=1, source_target_pairs={{0,16},{16,32},{32,48},{48,64},{64,80},{80,96},{96,112},{112,128},... | collective-permute-start | bytes 786440 | tf_op jit(solution)/shard_map/ppermute | solution.py:17
  337.5 53.3 %collective-permute-start.1 = (bf16[2,256,256]{1,2,0:T(8,128)(2,1)}, bf16[2,256,256]{1,2,0:T(8,128)(2,1)}, u32[]{:S(2)}, u32[]{:S(2)}) collective-permute-start(bf16[2,256,256]{1,2,0:T(8,128)(2,1)} %get-tuple-element.79), channel_id=1, source_target_pairs={{16,0},{32,16},{48,32},{64,48},{80,64},{96,80},{112,96},{128,112},... | collective-permute-start | bytes 786440 | tf_op jit(solution)/shard_map/ppermute | solution.py:20
  366.1 20.1 %copy-start.10 = (f32[16,2,128]{2,1,0:T(2,128)}, f32[16,2,128]{2,1,0:T(2,128)S(1)}, u32[]{:S(2)}) copy-start(f32[16,2,128]{2,1,0:T(2,128)S(1)} %all-gather.3) | copy-start | bytes 49156
  385.6 0.6 copy-start.11
  406.8 2.3 copy-start.3
  406.8 2.3 copy-start.13
  409.2 5.8 slice-start.1
  409.2 5.8 slice-start.2
  409.2 5.8 copy-start.12
  411.9 3.1 slice-start
  432.0 76.1 %copy-start.8 = (s32[4096]{0:T(1024)S(1)}, s32[4096]{0:T(1024)}, u32[]{:S(2)}) copy-start(s32[4096]{0:T(1024)} %broadcast_clamp_fusion) | copy-start | bytes 49156
  565.0 9.8 %copy-start.7 = (pred[1,6,32,128]{3,1,2,0:T(8,128)(4,1)S(1)}, pred[1,6,32,128]{3,1,2,0:T(8,128)(4,1)}, u32[]{:S(2)}) copy-start(pred[1,6,32,128]{3,1,2,0:T(8,128)(4,1)} %copy.235) | copy-start | bytes 73732
  574.8 7.8 %copy-start.4 = (f32[6,2,128,128]{2,3,0,1:T(8,128)S(1)}, f32[6,2,128,128]{2,3,0,1:T(8,128)}, u32[]{:S(2)}) copy-start(f32[6,2,128,128]{2,3,0,1:T(8,128)} %get-tuple-element.87) | copy-start | bytes 2359300
  574.8 7.9 %copy-start.1 = (f32[6,2,128,640]{3,2,1,0:T(8,128)S(1)}, f32[6,2,128,640]{3,2,1,0:T(8,128)}, u32[]{:S(2)}) copy-start(f32[6,2,128,640]{3,2,1,0:T(8,128)} %get-tuple-element.91) | copy-start | bytes 11796484
  583.9 13.8 %copy-start.5 = (bf16[1,4096,256]{1,2,0:T(8,128)(2,1)S(1)}, bf16[1,4096,256]{1,2,0:T(8,128)(2,1)}, u32[]{:S(2)}) copy-start(bf16[1,4096,256]{1,2,0:T(8,128)(2,1)} %copy.160) | copy-start | bytes 6291460
  608.3 3.2 copy-start.9
  611.5 0.9 copy-start.16
  611.5 0.9 copy-start.18
  611.5 0.9 copy-start.19
Sparse Core Ops, SparseCore 0:
  9.1 156.2 all-gather.8
  176.6 143.6 all-reduce.1
  324.4 55.9 all-gather.12
  383.3 93.8 all-gather.10
  617.7 137.3 reduce-scatter.1
where the time goes:
time: 764 us; the launch traced here: 762 us
  waiting for transfers between devices  485 us (63%)
  local copies, waits for them, and re-layouts  129 us (17%)
  blocking collectives  45.8 us (6%)
  matrix products  44.8 us (6%)
  other arithmetic  40.8 us (5%)
  between operations  13.7 us (2%)
    all_gather x1, waiting for transfers between devices, on_device(): piece = lax.all_gather(activations, 'heads', axis=1, tiled=True)  157 us
    psum x1, waiting for transfers between devices, on_device(): shared = lax.psum(chosen_rows.astype(jnp.bfloat16), 'seq')  144 us
    reduce_scatter x1, waiting for transfers between devices, on_device(): lax.psum_scatter(term.astype(jnp.bfloat16), 'heads', scatter_dimension=1,...  137 us
    all_gather x2, blocking collectives, combined_all(): pieces = jax.tree.map(lambda part: lax.all_gather(part, axis), value)  45.8 us
    all_gather x1, waiting for transfers between devices, on_device(): piece = lax.all_gather(stacked, 'seq', axis=1, tiled=True)  45.2 us
    gather x1, local copies, waits for them, and re-layouts, on_device(): chosen = piece[:, jnp.clip(offset_rows, 0, count - 1).reshape(-1)]  37.2 us
    all_gather x1, local copies, waits for them, and re-layouts, on_device(): piece = lax.all_gather(stacked, 'seq', axis=1, tiled=True)  30.9 us
    slice x2, local copies, waits for them, and re-layouts, on_device(): chosen[0]  19.7 us
  transfers between devices with their start and end apart: 7, of which 4 were waited for; matrix products, arithmetic and copies ran while one was open for 8% of the time, Pallas kernels for 0%

commit v1 on v0

--- a/solution.py
+++ b/solution.py
@@ -119,7 +119,16 @@
     slot_live = jnp.any(hits, axis=0)
     row_steps = jnp.arange(block_rows, dtype=jnp.int32)
     owner_ids = jnp.arange(blocks_here, dtype=jnp.int32)
-    piece = lax.all_gather(stacked, "seq", axis=1, tiled=True)
+    list_the_counts = lambda slab_in, ndim_at: jnp.concatenate(
+        lax.all_to_all(
+            jnp.stack(lax.axis_size("seq") * [slab_in]),
+            axis_name="seq",
+            split_axis=0,
+            concat_axis=0,
+        ),
+        axis=ndim_at,
+    )
+    piece = list_the_counts(stacked, 1)
     count = piece.shape[1]
     picked = slot_request.reshape(-1)
     alive = slot_live.reshape(-1)

time: 764 us -> 913 us (1.20)
  local copies, waits for them, and re-layouts: 129 us -> 193 us
  waiting for transfers between devices: 485 us -> 548 us
  starting transfers between devices: 2.62 us -> 15.3 us
    psum x1, waiting for transfers between devices: 144 us -> 257 us  [on_device(): shared = lax.psum(chosen_rows.astype(jnp.bfloat16), 'seq')]
    reshape x0 -> x1, local copies, waits for them, and re-layouts: none -> 80.2 us  [on_device(): jnp.concatenate(lax.all_to_all(jnp.stack(lax.axis_size('seq') * [slab_in]...]
    all_gather x1 -> x0, waiting for transfers between devices: 45.2 us -> none  [on_device(): piece = lax.all_gather(stacked, 'seq', axis=1, tiled=True)]
    all_gather x1 -> x0, local copies, waits for them, and re-layouts: 30.9 us -> none  [on_device(): piece = lax.all_gather(stacked, 'seq', axis=1, tiled=True)]
    all_to_all x0 -> x1, starting transfers between devices: none -> 12.7 us  [on_device(): lax.all_to_all(jnp.stack(lax.axis_size('seq') * [slab_in]), axis_name='se...]
  transfers between devices with their start and end apart: 7 -> 7, of which waited for: 4 -> 3; matrix products, arithmetic and copies ran while one was open for 8% -> 8% of each run, Pallas kernels for 0% -> 0%
where the time goes in v1:
time: 913 us; the launch traced here: 903 us
  waiting for transfers between devices  548 us (60%)
  local copies, waits for them, and re-layouts  193 us (21%)
  blocking collectives  47.1 us (5%)
  matrix products  44.8 us (5%)
  other arithmetic  40.1 us (4%)
  starting transfers between devices  15.3 us (2%)
  between operations  14.1 us (2%)
    psum x1, waiting for transfers between devices, on_device(): shared = lax.psum(chosen_rows.astype(jnp.bfloat16), 'seq')  257 us
    all_gather x1, waiting for transfers between devices, on_device(): piece = lax.all_gather(activations, 'heads', axis=1, tiled=True)  152 us
    reduce_scatter x1, waiting for transfers between devices, on_device(): lax.psum_scatter(term.astype(jnp.bfloat16), 'heads', scatter_dimension=1,...  139 us
    reshape x1, local copies, waits for them, and re-layouts, on_device(): jnp.concatenate(lax.all_to_all(jnp.stack(lax.axis_size('seq') * [slab_in]...  80.2 us
    all_gather x2, blocking collectives, combined_all(): pieces = jax.tree.map(lambda part: lax.all_gather(part, axis), value)  47.1 us
    gather x1, local copies, waits for them, and re-layouts, on_device(): chosen = piece[:, jnp.clip(offset_rows, 0, count - 1).reshape(-1)]  37.1 us
    slice x2, local copies, waits for them, and re-layouts, on_device(): chosen[0]  19.9 us
  transfers between devices with their start and end apart: 7, of which 3 were waited for; matrix products, arithmetic and copies ran while one was open for 8% of the time, Pallas kernels for 0%

profile of v1, /device:TPU:1, one launch (start us, length us, event | category | flops | bytes accessed | tf_op | source)
XLA Modules:
  0.0 902.7 jit_solution(4159118868242883362)
XLA Ops:
  7.3 0.7 broadcast_compare_fusion.1
  8.7 0.8 copy.127
  13.7 151.7 %all-gather.8.cloned.1.call-done = bf16[768,4096]{1,0:T(8,128)(2,1)} async-done(((bf16[768,256]{1,0:T(8,128)(2,1)}), bf16[768,4096]{1,0:T(8,128)(2,1)}) %all-gather.8.cloned.1.call-update) | async-done | bytes 6291472 | tf_op jit(solution)/shard_map/all_gather | solution.py:71
  165.4 5.4 convolution_convert_fusion.1
  171.2 2.0 convolution_convert_fusion.2
  173.2 2.0 convolution_convert_fusion.3
  175.2 1.2 fusion.43
  176.6 1.0 pad_maximum_fusion.1
  177.6 1.4 copy.131
  179.0 5.9 stack.11
  184.9 12.7 %all-to-all-start = ((bf16[16,2,768,256]{3,2,1,0:T(8,128)(2,1)}), bf16[16,2,768,256]{3,2,1,0:T(8,128)(2,1)}, u32[]{:S(2)}, u32[]{:S(2)}) async-start(bf16[16,2,768,256]{3,2,1,0:T(8,128)(2,1)} %stack.11), calls=%async_computation | async-start | bytes 25165824 | tf_op jit(solution)/shard_map/all_to_all | solution.py:123
  197.7 256.8 %all-reduce.2.cloned.1.call-done = bf16[128,768]{1,0:T(8,128)(2,1)} async-done(((bf16[128,768]{1,0:T(8,128)(2,1)}), bf16[128,768]{1,0:T(8,128)(2,1)}) %all-reduce.2.cloned.1.call-update) | async-done | bytes 196624 | tf_op jit(solution)/shard_map/psum | solution.py:161
  454.5 1.6 fusion.95
  456.1 1.3 fusion.96
  457.5 1.0 fusion.55
  459.1 1.9 copy.123
  461.1 1.8 reshape.317
  462.9 1.8 fusion.67
  465.2 2.0 collective-permute-start.1
  467.2 27.8 %all-gather.3 = f32[16,2,128]{2,1,0:T(2,128)S(1)} all-gather(f32[1,2,128]{2,1,0:T(2,128)S(1)} %bitcast.212), channel_id=2, replica_groups=mesh['seq'=16,'heads'=16] {'seq'}, dimensions={0}, use_global_device_ids=true | all-gather | bytes 17408 | tf_op jit(solution)/shard_map/all_gather | solution.py:26
  495.3 19.3 %all-gather.4 = f32[16,2,128]{2,1,0:T(2,128)S(1)} all-gather(f32[1,2,128]{2,1,0:T(2,128)S(1)} %bitcast.213), channel_id=3, replica_groups=mesh['seq'=16,'heads'=16] {'seq'}, dimensions={0}, use_global_device_ids=true | all-gather | bytes 17408 | tf_op jit(solution)/shard_map/all_gather | solution.py:26
  515.1 1.6 copy.170
  516.7 0.9 reshape.323
  517.6 2.2 fusion.97
  519.7 2.3 pad_maximum_fusion
  522.0 2.6 copy.124
  524.6 2.9 reshape.318
  528.2 0.7 fusion.49
  529.0 0.7 fusion.48
  529.7 0.7 fusion.47
  530.4 0.7 fusion.46
  531.1 4.7 fusion.94
  535.8 1.8 copy.142
  538.1 2.7 fusion.8
  540.9 3.0 slice.104
  543.9 16.7 %while.14 = (s32[]{:T(128)}, f32[2,128]{1,0:T(2,128)S(1)}, f32[2,128]{1,0:T(2,128)S(1)}, f32[2,128,128]{2,1,0:T(8,128)S(1)}, f32[15,2,128]{2,1,0:T(2,128)S(1)}, ...) while((s32[]{:T(128)}, f32[2,128]{1,0:T(2,128)S(1)}, f32[2,128]{1,0:T(2,128)S(1)}, ...), condition=%wide.region_5.6_spmd, body=%wide.region_4.5_spmd.sunk | while | flops 99842 | bytes 403557 | solution.py:29
  543.9 1.1 fusion.117
  545.1 1.1 fusion.117
  546.2 1.1 fusion.117
  547.3 1.1 fusion.117
  548.4 1.1 fusion.117
  549.5 1.1 fusion.117
  550.6 1.1 fusion.117
  551.8 1.1 fusion.117
  552.9 1.1 fusion.117
  554.0 1.1 fusion.117
  555.1 1.1 fusion.117
  556.2 1.1 fusion.117
  557.3 1.1 fusion.117
  558.4 1.1 fusion.117
  559.6 1.1 fusion.117
  560.9 6.5 copy.132
  567.4 80.2 %copy.134 = bf16[2,12288,256]{2,0,1:T(2,128)(2,1)} copy(bf16[2,12288,256]{2,1,0:T(8,128)(2,1)S(1)} %bitcast.186) | data formatting | bytes 25165824 | tf_op jit(solution)/shard_map/reshape | solution.py:122
  647.6 37.1 %gather_fusion.1 = bf16[4096,2,256]{2,1,0:T(2,128)(2,1)} fusion(bf16[2,12288,256]{2,0,1:T(2,128)(2,1)} %copy.134, s32[4096]{0:T(1024)S(1)} %copy-done.8), kind=kCustom, calls=%fused_computation.1 | custom fusion | bytes 8404992 | tf_op jit(solution)/shard_map/gather | solution.py:137
  684.7 10.0 %fusion.93 = (bf16[1,4096,256]{2,0,1:T(2,128)(2,1)}, bf16[1,4096,256]{2,0,1:T(2,128)(2,1)}) fusion(bf16[2,4096,256]{2,0,1:T(2,128)(2,1)} %bitcast.187), kind=kLoop, calls=%fused_computation.149 | loop fusion | bytes 8388608 | tf_op jit(solution)/shard_map/slice | solution.py:140
  694.7 9.9 %copy.135 = bf16[1,4096,256]{1,2,0:T(8,128)(2,1)} copy(bf16[1,4096,256]{2,0,1:T(2,128)(2,1)} %get-tuple-element.72) | data formatting | bytes 4194304 | tf_op jit(solution)/shard_map/slice | solution.py:140
  704.6 9.8 %copy.143 = bf16[1,4096,256]{1,2,0:T(8,128)(2,1)} copy(bf16[1,4096,256]{2,0,1:T(2,128)(2,1)} %get-tuple-element.73) | data formatting | bytes 4194304 | tf_op jit(solution)/shard_map/slice | solution.py:150
  714.4 7.7 fusion.3
  722.3 1.2 fusion.9
  723.5 13.6 %fusion.4 = (f32[6,2,128]{2,0,1:T(8,128)S(1)}, bf16[6,2,128,4096]{2,3,0,1:T(8,128)(2,1)}) fusion(f32[2,4096,6,128]{3,1,2,0:T(8,128)S(1)} %get-tuple-element.89, f32[6,2,128]{2,0,1:T(8,128)S(1)} %copy.145, pred[6,4096]{1,0:T(8,128)(4,1)S(1)} %bitcast.204), kind=kLoop, calls=%fused_computation.14 | loop fusion | flops 37747200 | bytes 37785600 | tf_op jit(solution)/shard_map/reduce_sum | solution.py:41
  737.1 10.6 %fusion.18 = f32[6,128,2,128]{3,1,2,0:T(8,128)} fusion(bf16[4096,2,128,1]{0,2,1,3:T(8,128)(2,1)S(1)} %bitcast.198, bf16[6,2,128,4096]{2,3,0,1:T(8,128)(2,1)} %get-tuple-element.71), kind=kOutput, calls=%fused_computation.31 | convolution fusion | flops 1610612736 | bytes 15466496 | tf_op jit(solution)/shard_map/bhqk,khd->bhqd/dot_general | solution.py:150
  747.7 3.2 fusion.33
  752.4 4.5 convolution_convert_fusion
  756.9 138.8 %reduce-scatter.2.cloned.1.call-done = bf16[768,256]{1,0:T(8,128)(2,1)} async-done(((bf16[768,4096]{1,0:T(8,128)(2,1)}), bf16[768,256]{1,0:T(8,128)(2,1)}) %reduce-scatter.2.cloned.1.call-update) | async-done | bytes 393232 | tf_op jit(solution)/shard_map/reduce_scatter | solution.py:200
  (125 shorter events, 11.6 us)
Async XLA Ops:
  6.5 745.9 %copy-start = (bf16[256,4096]{1,0:T(8,128)(2,1)S(1)}, bf16[256,4096]{1,0:T(8,128)(2,1)}, u32[]{:S(2)}) copy-start(bf16[256,4096]{1,0:T(8,128)(2,1)} %param.14) | copy-start | bytes 6291460
  6.5 158.8 %all-gather.8.cloned.1.call-start = ((), (), s32[]{:S(2)}) async-start(), calls=%async_computation.2 | async-start | bytes 6684672 | tf_op jit(solution)/shard_map/all_gather | solution.py:71
  7.3 447.3 %all-reduce.2.cloned.1.call-start = ((), (), s32[]{:S(2)}) async-start(), calls=%async_computation.3 | async-start | bytes 393216 | tf_op jit(solution)/shard_map/psum | solution.py:161
  13.0 163.5 %copy-start.13 = (pred[128]{0:T(512)(128)(4,1)}, pred[128]{0:T(512)(128)(4,1)S(1)}, u32[]{:S(2)}) copy-start(pred[128]{0:T(512)(128)(4,1)S(1)} %get-tuple-element.68) | copy-start | bytes 388
  13.0 163.5 %copy-start.15 = (s32[128]{0:T(128)}, s32[128]{0:T(128)S(1)}, u32[]{:S(2)}) copy-start(s32[128]{0:T(128)S(1)} %get-tuple-element.69) | copy-start | bytes 1540
  165.4 5.4 copy-start.18
  165.4 5.8 copy-start.19
  171.2 2.0 copy-start.20
  173.2 3.4 copy-start.2
  175.2 1.4 copy-start.6
  184.9 375.9 %all-to-all-start = ((bf16[16,2,768,256]{3,2,1,0:T(8,128)(2,1)}), bf16[16,2,768,256]{3,2,1,0:T(8,128)(2,1)}, u32[]{:S(2)}, u32[]{:S(2)}) async-start(bf16[16,2,768,256]{3,2,1,0:T(8,128)(2,1)} %stack.11), calls=%async_computation | async-start | bytes 25165824 | tf_op jit(solution)/shard_map/all_to_all | solution.py:123
  197.7 343.2 %all-gather.10.cloned.1.call-start = ((), (), s32[]{:S(2)}) async-start(), calls=%async_computation.5 | async-start | bytes 2228224 | tf_op jit(solution)/shard_map/all_gather | solution.py:26
  458.5 437.2 %reduce-scatter.2.cloned.1.call-start = ((), (), s32[]{:S(2)}) async-start(), calls=%async_computation.4 | async-start | bytes 6684672 | tf_op jit(solution)/shard_map/reduce_scatter | solution.py:200
  464.7 55.0 %collective-permute-start = (bf16[2,256,256]{1,2,0:T(8,128)(2,1)}, bf16[2,256,256]{1,2,0:T(8,128)(2,1)S(1)}, u32[]{:S(2)}, u32[]{:S(2)}) collective-permute-start(bf16[2,256,256]{1,2,0:T(8,128)(2,1)} %get-tuple-element.78), channel_id=1, source_target_pairs={{0,16},{16,32},{32,48},{48,64},{64,80},{80,96},{96,112},{112,128},... | collective-permute-start | bytes 786440 | tf_op jit(solution)/shard_map/ppermute | solution.py:17
  465.2 54.6 %collective-permute-start.1 = (bf16[2,256,256]{1,2,0:T(8,128)(2,1)}, bf16[2,256,256]{1,2,0:T(8,128)(2,1)}, u32[]{:S(2)}, u32[]{:S(2)}) collective-permute-start(bf16[2,256,256]{1,2,0:T(8,128)(2,1)} %get-tuple-element.79), channel_id=1, source_target_pairs={{16,0},{32,16},{48,32},{64,48},{80,64},{96,80},{112,96},{128,112},... | collective-permute-start | bytes 786440 | tf_op jit(solution)/shard_map/ppermute | solution.py:20
  495.0 19.5 %copy-start.10 = (f32[16,2,128]{2,1,0:T(2,128)}, f32[16,2,128]{2,1,0:T(2,128)S(1)}, u32[]{:S(2)}) copy-start(f32[16,2,128]{2,1,0:T(2,128)S(1)} %all-gather.3) | copy-start | bytes 49156
  514.5 0.6 copy-start.11
  535.8 2.3 copy-start.3
  535.8 2.3 copy-start.12
  538.1 5.8 slice-start.1
  538.1 5.8 slice-start.2
  540.9 3.0 slice-start
  567.4 80.2 %copy-start.8 = (s32[4096]{0:T(1024)S(1)}, s32[4096]{0:T(1024)}, u32[]{:S(2)}) copy-start(s32[4096]{0:T(1024)} %broadcast_clamp_fusion) | copy-start | bytes 49156
  704.6 9.8 %copy-start.7 = (pred[1,6,32,128]{3,1,2,0:T(8,128)(4,1)S(1)}, pred[1,6,32,128]{3,1,2,0:T(8,128)(4,1)}, u32[]{:S(2)}) copy-start(pred[1,6,32,128]{3,1,2,0:T(8,128)(4,1)} %copy.218) | copy-start | bytes 73732
  714.4 7.8 copy-start.4
  714.4 7.9 copy-start.1
  723.5 13.6 %copy-start.5 = (bf16[1,4096,256]{1,2,0:T(8,128)(2,1)S(1)}, bf16[1,4096,256]{1,2,0:T(8,128)(2,1)}, u32[]{:S(2)}) copy-start(bf16[1,4096,256]{1,2,0:T(8,128)(2,1)} %copy.143) | copy-start | bytes 6291460
  747.7 3.2 copy-start.9
  750.9 0.9 copy-start.14
  750.9 0.9 copy-start.16
  750.9 0.9 copy-start.17
Sparse Core Ops, SparseCore 0:
  9.1 156.2 all-gather.7
  176.6 277.9 all-reduce.1
  458.6 54.5 all-gather.9
  757.1 138.6 reduce-scatter.1
